TPU v7x, 32 devices: a whole 2x2x4 slice. The times are simulated.
32 devices in a mesh: pulse: 4 (over z), tile: 8 (over y, x, core).
Axes of the slice: x: 2, y: 2, z: 4, core: 2. Of those that a mesh axis runs over, the one named last changes fastest.
Arguments:
- raw: bfloat16 [2, 128, 2048], P(None, ('pulse', 'tile')), may hold values from -6 to 6
- filt: bfloat16 [2, 1024, 2048], replicated, may hold values from -0.125 to 0.125
- range_off: int32 [128], P(('pulse', 'tile')), may hold values from 0 to 1024
- fine: int32 [128], P(('pulse', 'tile')), may hold values from 0 to 3
- dop: int32 [128], P(('pulse', 'tile')), may hold values from 0 to 511
- pulse_order: int32 [32, 4], P(('pulse', 'tile')), may hold values from 0 to 3, each once within a row
- band_idx: int32 [8, 128], P(None, ('pulse', 'tile')), may hold values from 0 to 1023
Outputs:
- image: bfloat16 [2, 512, 32768], P(None, 'pulse', 'tile')
Inputs may be any that keep to these rules, and one draw needn't show every extreme that they name: `pulse_order`: each row is a permutation of 0 .. 3.
All inputs are finite; a program needn't handle non-finite values.
Results may differ from a plain program's by a relative error of at most 0.0065.
Values may be sent and summed in bfloat16 or wider, within the bound.
A program may use at most 192 MiB of HBM per device.

v0:
```python
import functools

import jax
import jax.numpy as jnp
from jax import lax
from jax.experimental import pallas as pl
from jax.experimental.pallas import tpu as pltpu
from jax.sharding import PartitionSpec as P

F32 = jnp.float32
BF16 = jnp.bfloat16
MESH = pl.DeviceIdType.MESH
LANES = 128
DOP_SPLIT = 32
VMEM_LIMIT = 60 * 1024 * 1024


def spread(meta, field, rows8, n_rows):
    lane = lax.broadcasted_iota(jnp.int32, (meta.shape[1], n_rows), 0)
    col = lax.broadcasted_iota(jnp.int32, (meta.shape[1], n_rows), 1)
    pick = (lane == field * rows8 + col % rows8).astype(F32).astype(BF16)
    wide = jnp.dot(meta, pick, preferred_element_type=F32)
    owner = lax.broadcasted_iota(jnp.int32, wide.shape, 0)
    column = lax.broadcasted_iota(jnp.int32, wide.shape, 1)
    return jnp.sum(jnp.where(owner == column // rows8, wide, 0.0), axis=0, keepdims=True)


def thirds(x):
    a = x.astype(BF16)
    rest = x - a.astype(F32)
    b = rest.astype(BF16)
    return [a, b, (rest - b.astype(F32)).astype(BF16)]


def swap_parts(v, part1, p_dev):
    n = v.shape[-1]
    return jnp.where(part1, pltpu.roll(v, p_dev, 1), pltpu.roll(v, n - p_dev, 1))


def focus_kernel(
    n_pulse, n_tile, r_dev,
    off_ref, fine_ref, dop_ref, order_ref, idx_ref, raw_ref, filt_ref,
    left_ref, bands_ref,
    win_ref, meta_ref, scal_ref, filt_buf, x_ref, prof_ref, cut_ref, out_buf, g_ref, got_ref,
    f_sem, s_sem, z_send, z_recv, t_send, t_recv, p_send, p_recv, g_send, g_recv,
):
    me_p = lax.axis_index("pulse")
    me_t = lax.axis_index("tile")
    half = n_tile // 2
    core = me_t % 2
    chip = me_t // 2
    partner = chip * 2 + (1 - core)
    p_dev = raw_ref.shape[1]
    steps = order_ref.shape[1]
    raw_len = raw_ref.shape[2]
    win = x_ref.shape[2]
    rows = x_ref.shape[1]
    rows8 = 2 * p_dev
    n_dev = n_pulse * half
    n_rows = 2 * rows
    chunks, chunk = filt_buf.shape[0], filt_buf.shape[3]
    stride = prof_ref.shape[0] // rows
    band = bands_ref.shape[3]
    pieces = band // LANES

    def pulse_peer(d):
        return (lax.rem(me_p + d, n_pulse), me_t)

    def tile_peer(d):
        return (me_p, lax.rem(chip + d, half) * 2 + core)

    def any_tile(d):
        return (me_p, lax.rem(me_t + d, n_tile))

    barrier = pltpu.get_barrier_semaphore()
    for d in range(1, n_pulse):
        pl.semaphore_signal(barrier, 1, device_id=pulse_peer(d), device_id_type=MESH)
    for d in range(1, n_tile):
        pl.semaphore_signal(barrier, 1, device_id=any_tile(d), device_id_type=MESH)

    def load_filter(n):
        return pltpu.make_async_copy(
            filt_ref.at[:, :, pl.ds(n * chunk, chunk)], filt_buf.at[n], f_sem.at[n]
        )

    for n in range(chunks):
        load_filter(n).start()

    raw = jnp.concatenate([raw_ref[0].astype(F32), raw_ref[1].astype(F32)], 0)
    row = lax.broadcasted_iota(jnp.int32, (rows8, win), 0)
    cut = jnp.zeros((rows8, win), F32)
    for p in range(p_dev):
        off = off_ref[p]
        shift = jnp.where(off == 0, 0, raw_len - off)
        turned = pltpu.roll(raw, shift, 1)[:, :win]
        cut = jnp.where(row % p_dev == p, turned, cut)
    mine = me_p * half + chip
    win_ref[mine] = cut.astype(BF16)
    lane = lax.broadcasted_iota(jnp.int32, meta_ref.shape[2:], 1)
    line = jnp.zeros(meta_ref.shape[2:], jnp.int32)
    for p in range(p_dev):
        pulse_lane = (lane < 4 * rows8) & (lane % p_dev == p)
        line = jnp.where(pulse_lane & (lane // rows8 == 1), fine_ref[p], line)
        line = jnp.where(pulse_lane & (lane // rows8 == 2), dop_ref[p] % DOP_SPLIT, line)
        line = jnp.where(pulse_lane & (lane // rows8 == 3), dop_ref[p] // DOP_SPLIT, line)
        line = jnp.where((lane < rows8) & (lane % p_dev == order_ref[0, p]), p, line)
        for t in range(n_tile):
            line = jnp.where(lane == 4 * rows8 + t * p_dev + p, idx_ref[t, p], line)
    meta_ref[core, mine] = line
    pl.semaphore_wait(barrier, n_pulse - 1 + n_tile - 1)

    def copies(slot, send, recv, at, target):
        return [
            pltpu.make_async_remote_copy(
                src_ref=ref, dst_ref=ref, send_sem=send.at[(a,) + at], recv_sem=recv.at[(a,) + at],
                device_id=target, device_id_type=MESH,
            )
            for a, ref in enumerate((win_ref.at[slot], meta_ref.at[core, slot]))
        ]

    started = []

    def send(*args):
        for c in copies(*args):
            c.start()
            started.append(c)

    def arrive(*args):
        for c in copies(*args):
            c.wait_recv()

    for d in reversed(range(1, n_pulse)):
        send(mine, z_send, z_recv, (d,), pulse_peer(d))
    for dp in range(n_pulse):
        slot = lax.rem(me_p + n_pulse - dp, n_pulse) * half + chip
        if dp:
            arrive(slot, z_send, z_recv, (dp,), pulse_peer(dp))
        for dt in reversed(range(1, half)):
            send(slot, t_send, t_recv, (dp, dt), tile_peer(dt))
    for dp in range(n_pulse):
        for dt in range(1, half):
            slot = lax.rem(me_p + n_pulse - dp, n_pulse) * half + lax.rem(chip + half - dt, half)
            arrive(slot, t_send, t_recv, (dp, dt), tile_peer(dt))

    to_scalar = pltpu.make_async_copy(meta_ref.at[core], scal_ref, s_sem)
    to_scalar.start()
    meta_move = pltpu.make_async_remote_copy(
        src_ref=meta_ref.at[core], dst_ref=meta_ref.at[core],
        send_sem=p_send.at[2], recv_sem=p_recv.at[2],
        device_id=(me_p, partner), device_id_type=MESH,
    )
    meta_move.start()
    x = win_ref[...].astype(F32)
    r = lax.broadcasted_iota(jnp.int32, x.shape, 1)
    y = jnp.where(r < p_dev, -1.0, 1.0) * pltpu.roll(x, p_dev, 1)
    x_ref[0] = x.reshape(rows, win).astype(BF16)
    x_ref[1] = y.reshape(rows, win).astype(BF16)

    def compress(n, carry):
        load_filter(n).wait()
        acc = jnp.dot(x_ref[0], filt_buf[n, 0], preferred_element_type=F32) + jnp.dot(
            x_ref[1], filt_buf[n, 1], preferred_element_type=F32
        )
        acc = acc.astype(BF16).astype(F32)
        for c in range(chunk // LANES):
            prof_ref[pl.ds(n * (chunk // LANES) + c, rows, stride=stride), :] = acc[
                :, c * LANES : (c + 1) * LANES
            ]
        return carry

    lax.fori_loop(0, chunks, compress, 0)
    to_scalar.wait()
    lane8 = lax.broadcasted_iota(jnp.int32, (pieces, LANES), 1)

    def cut_bands(tile):
        def owner(d, carry):
            for p in range(p_dev):
                start = scal_ref[d, 0, 4 * rows8 + tile * p_dev + p]
                q = start >> 7
                r = start & (LANES - 1)
                turn = (LANES - r) & (LANES - 1)
                keep = lane8 < LANES - r
                for part in range(2):
                    row = d * rows8 + part * p_dev + p
                    low = pltpu.roll(prof_ref[pl.ds(row * stride + q, pieces), :], turn, 1)
                    high = pltpu.roll(prof_ref[pl.ds(row * stride + q + 1, pieces), :], turn, 1)
                    here = jnp.where(keep, low, high)
                    after = pltpu.roll(jnp.where(lane8 == 0, high, here), LANES - 1, 1)
                    cut_ref[pl.ds(row * pieces, pieces), :] = here
                    cut_ref[pl.ds((rows + row) * pieces, pieces), :] = after
            return carry

        lax.fori_loop(0, n_dev, owner, 0, unroll=4)

    cut_bands(partner)
    for c in range(pieces):
        for b in range(2):
            out_buf[b, :, c * LANES : (c + 1) * LANES] = cut_ref[
                pl.ds(b * rows * pieces + c, rows, stride=pieces), :
            ].astype(BF16)
    band_moves = [
        pltpu.make_async_remote_copy(
            src_ref=out_buf.at[b], dst_ref=bands_ref.at[b, core],
            send_sem=p_send.at[b], recv_sem=p_recv.at[b],
            device_id=(me_p, partner), device_id_type=MESH,
        )
        for b in range(2)
    ]
    for move in band_moves:
        move.start()
    cut_bands(me_t)
    for c in range(pieces):
        for b in range(2):
            bands_ref[b, core, :, c * LANES : (c + 1) * LANES] = cut_ref[
                pl.ds(b * rows * pieces + c, rows, stride=pieces), :
            ].astype(BF16)
    pltpu.make_async_remote_copy(
        src_ref=meta_ref.at[1 - core], dst_ref=meta_ref.at[1 - core],
        send_sem=p_send.at[2], recv_sem=p_recv.at[2],
        device_id=(me_p, partner), device_id_type=MESH,
    ).wait_recv()
    meta = meta_ref[...].reshape(2 * n_dev, meta_ref.shape[3]).astype(F32).astype(BF16)
    blk = spread(meta, 0, rows8, n_rows)
    fine = spread(meta, 1, rows8, n_rows) * (1.0 / 16.0)
    dop = spread(meta, 2, rows8, n_rows) + DOP_SPLIT * spread(meta, 3, rows8, n_rows)
    sel = lax.broadcasted_iota(jnp.int32, (2 * steps, n_rows), 0)
    col = lax.broadcasted_iota(jnp.int32, (2 * steps, n_rows), 1)
    in_block = (sel // 2).astype(F32) == blk
    same = in_block & (sel % 2 == (col % rows8) // p_dev)
    zero = jnp.zeros((2 * steps, n_rows), F32)
    p_left = jnp.concatenate([jnp.where(same, 1.0 - fine, zero), jnp.where(same, fine, zero)], 1)
    q_left = jnp.concatenate([jnp.where(same, -1.0, zero), jnp.where(same, 1.0, zero)], 1)
    left = jnp.concatenate([p_left, q_left], 0).astype(BF16)
    for b in range(2):
        pltpu.make_async_remote_copy(
            src_ref=out_buf.at[b], dst_ref=bands_ref.at[b, 1 - core],
            send_sem=p_send.at[b], recv_sem=p_recv.at[b],
            device_id=(me_p, partner), device_id_type=MESH,
        ).wait_recv()
    bands = bands_ref[...].reshape(2 * n_rows, band)
    pq = jnp.dot(left, bands, preferred_element_type=F32)
    k = 2 * steps
    x = 4.0 * pq[:k] + 1.5 * pq[k:]
    y = 1.5 * pq[:k] + 0.875 * pq[k:]
    xs = jnp.concatenate(thirds(x) + thirds(y), 0)
    d6 = lax.dot_general(xs, bands, (((1,), (1,)), ((), ())), preferred_element_type=F32)
    dx = d6[2 * k : 3 * k] + d6[k : 2 * k] + d6[:k]
    dy = d6[5 * k : 6 * k] + d6[4 * k : 5 * k] + d6[3 * k : 4 * k]
    h = ((1.0 - fine) * dx[:, :n_rows] - dy[:, :n_rows]) + (
        fine * dx[:, n_rows:] + dy[:, n_rows:]
    )
    hr = jnp.sum(jnp.where(in_block & (sel % 2 == 0), h, 0.0), axis=0, keepdims=True)
    hi = jnp.sum(jnp.where(in_block & (sel % 2 == 1), h, 0.0), axis=0, keepdims=True)
    both = jnp.concatenate([hr, hi, jnp.zeros((6, n_rows), F32)], 0)
    part1 = (lax.broadcasted_iota(jnp.int32, (8, n_rows), 1) % rows8) >= p_dev
    other = swap_parts(both, part1, p_dev)
    hr, hi, hr_o, hi_o = both[0:1], both[1:2], other[0:1], other[1:2]
    one = part1[0:1]
    g_ref[0:1] = jnp.where(one, hr_o + hi, hr + hi_o)
    g_ref[1:2] = jnp.where(one, hr - hi_o, hr_o - hi)
    g_moves = [
        pltpu.make_async_remote_copy(
            src_ref=g_ref, dst_ref=got_ref.at[d],
            send_sem=g_send.at[d], recv_sem=g_recv.at[d],
            device_id=any_tile(d), device_id_type=MESH,
        )
        for d in range(1, n_tile)
    ]
    for move in g_moves:
        move.start()
    total_rows = r_dev * n_pulse
    image_row = me_p * r_dev + lax.broadcasted_iota(jnp.int32, (r_dev, n_rows), 0)
    turns = dop.astype(jnp.int32) * image_row
    if total_rows & (total_rows - 1):
        turns = turns % total_rows
    else:
        turns = turns & (total_rows - 1)
    angle = 2.0 * jnp.pi * turns.astype(F32) / total_rows
    norm = 1.0 / jnp.sqrt(F32(n_rows // 2))
    er = (jnp.cos(angle) * norm).astype(BF16).astype(F32)
    ei = (jnp.sin(angle) * norm).astype(BF16).astype(F32)
    total = g_ref[...]
    for d in range(1, n_tile):
        g_moves[d - 1].wait_recv()
        total = total + got_ref[d]
    g_re, g_im = total[0:1], total[1:2]
    scale = jnp.sqrt(g_re * g_re + g_im * g_im + 1.0)
    c_re = g_re / scale
    c_im = -g_im / scale
    alpha = jnp.where(one, -c_im, c_re)
    beta = jnp.where(one, c_re, c_im)
    w = (er * alpha - ei * beta, er * beta + ei * alpha)
    for z in range(2):
        here = pl.ds(z * r_dev, r_dev)
        left_ref[0, here, :n_rows] = (w[z] * (1.0 - fine)).astype(BF16)
        left_ref[0, here, n_rows:] = (w[z] * fine).astype(BF16)
        left_ref[1, here, :n_rows] = (w[z] * -fine).astype(BF16)
        left_ref[1, here, n_rows:] = (w[z] * (1.0 + fine)).astype(BF16)
    for c in started + [meta_move] + band_moves + g_moves:
        c.wait_send()


def focus(n_pulse, n_tile, r_dev, band, range_off, fine, dop, order, idx, raw, filt):
    p_dev = raw.shape[1]
    win, ups = filt.shape[1:]
    half = n_tile // 2
    n_dev = n_pulse * half
    rows = n_dev * 2 * p_dev
    n_rows = 2 * rows
    fields = 8 * p_dev + idx.size
    width = fields + -fields % LANES
    chunk = 2 * LANES
    sem = pltpu.SemaphoreType.DMA
    return pl.pallas_call(
        functools.partial(focus_kernel, n_pulse, n_tile, r_dev),
        out_shape=(
            jax.ShapeDtypeStruct((2, 2 * r_dev, 2 * n_rows), BF16),
            jax.ShapeDtypeStruct((2, 2, rows, band), BF16),
        ),
        in_specs=[pl.BlockSpec(memory_space=pltpu.SMEM)] * 5
        + [pl.BlockSpec(memory_space=pltpu.VMEM), pl.BlockSpec(memory_space=pl.ANY)],
        out_specs=[pl.BlockSpec(memory_space=pltpu.VMEM)] * 2,
        scratch_shapes=[
            pltpu.VMEM((n_dev, 2 * p_dev, win), BF16),
            pltpu.VMEM((2, n_dev, 1, width), jnp.int32),
            pltpu.SMEM((n_dev, 1, width), jnp.int32),
            pltpu.VMEM((ups // chunk, 2, win, chunk), BF16),
            pltpu.VMEM((2, rows, win), BF16),
            pltpu.VMEM((rows * (ups // LANES) + 8, LANES), F32),
            pltpu.VMEM((2 * rows * (band // LANES), LANES), F32),
            pltpu.VMEM((2, rows, band), BF16),
            pltpu.VMEM((2, n_rows), F32),
            pltpu.VMEM((n_tile, 2, n_rows), F32),
            sem((ups // chunk,)),
            sem,
            sem((2, n_pulse)),
            sem((2, n_pulse)),
            sem((2, n_pulse, half)),
            sem((2, n_pulse, half)),
            sem((3,)),
            sem((3,)),
            sem((n_tile,)),
            sem((n_tile,)),
        ],
        compiler_params=pltpu.CompilerParams(
            collective_id=0, has_side_effects=True, vmem_limit_bytes=VMEM_LIMIT
        ),
    )(range_off, fine, dop, order, idx, raw, filt)


def image_kernel(left_ref, bands_ref, out_ref, up_ref):
    r_dev = out_ref.shape[1]
    width = bands_ref.shape[1]
    out_chunk = 4 * LANES
    j = lax.broadcasted_iota(jnp.int32, up_ref.shape, 0)
    c = lax.broadcasted_iota(jnp.int32, up_ref.shape, 1)
    w = (c % 4).astype(F32) * 0.25
    up = jnp.where(j < LANES, 1.0 - w, w)
    up_ref[...] = jnp.where(j % LANES == c // 4, up, 0.0).astype(BF16)
    r0 = jnp.dot(left_ref[0], bands_ref[...], preferred_element_type=F32).astype(BF16)
    r1 = jnp.dot(left_ref[1], bands_ref[...], preferred_element_type=F32).astype(BF16)
    for s in range(width // LANES):
        cols = slice(s * LANES, (s + 1) * LANES)
        both = jnp.concatenate([r0[:, cols], r1[:, cols]], 1)
        res = jnp.dot(both, up_ref[...], preferred_element_type=F32).astype(BF16)
        for z in range(2):
            out_ref[z, :, s * out_chunk : (s + 1) * out_chunk] = res[z * r_dev : (z + 1) * r_dev]


def image(left, bands, r_dev):
    band = bands.shape[1]
    k = bands.shape[0]
    width = 2 * LANES
    return pl.pallas_call(
        image_kernel,
        grid=(band // width,),
        out_shape=jax.ShapeDtypeStruct((2, r_dev, 4 * band), BF16),
        in_specs=[
            pl.BlockSpec(left.shape, lambda i: (0, 0, 0)),
            pl.BlockSpec((k, width), lambda i: (0, i)),
        ],
        out_specs=pl.BlockSpec((2, r_dev, 4 * width), lambda i: (0, 0, i)),
        scratch_shapes=[pltpu.VMEM((2 * LANES, 4 * LANES), BF16)],
        compiler_params=pltpu.CompilerParams(vmem_limit_bytes=VMEM_LIMIT),
    )(left, bands)


BAND = 1024
R_DEV = 128


def shards(raw, filt, range_off, fine, dop, pulse_order, band_idx):
    n_pulse = lax.axis_size("pulse")
    n_tile = lax.axis_size("tile")
    left, bands = focus(
        n_pulse, n_tile, R_DEV, BAND, range_off, fine, dop, pulse_order, band_idx, raw, filt
    )
    bands = bands.reshape(-1, BAND)
    return image(left, bands, R_DEV)


def solution(mesh):
    return jax.shard_map(
        shards,
        mesh=mesh,
        in_specs=(
            P(None, ("pulse", "tile"), None),
            P(),
            P(("pulse", "tile")),
            P(("pulse", "tile")),
            P(("pulse", "tile")),
            P(("pulse", "tile"), None),
            P(None, ("pulse", "tile")),
        ),
        out_specs=P(None, "pulse", "tile"),
        check_vma=False,
    )
```

profile of v0, /device:TPU:0, one launch (start us, length us, event | category | flops | bytes accessed | tf_op | source)
XLA Modules:
  0.0 31.7 jit_solution(13841057886798387479)
XLA Ops:
  0.0 1.3 %copy.8.idx_ref = s32[8,4]{1,0:T(8,128)} copy(s32[8,4]{0,1:T(4,128)} %param.13) | data formatting | bytes 256 | tf_op args[6]
  1.3 25.6 %shard_map.73 = (bf16[2,256,512]{2,1,0:T(8,128)(2,1)}, bf16[2,2,128,1024]{3,2,1,0:T(8,128)(2,1)}) custom-call(s32[4]{0:T(128)} %off_ref.1, s32[4]{0:T(128)} %fine_ref.1, s32[4]{0:T(128)} %dop_ref.1, s32[1,4]{1,0:T(1,128)} %order_ref.1, s32[8,4]{1,0:T(8,128)} %copy.8.idx_ref, bf16[2,4,2048]{2,1,0:T(4,128)(2,1)} %raw_ref.1, bf16[2,1024,2048]{2,1,0:T(8,128)(2,1)} %filt_ref.1), custom_call_target="tpu_custom_call" | custom-call | tf_op jit(solution)/shard_map/pallas_call | solution.py:314
  27.0 4.7 %shard_map.74 = bf16[2,128,4096]{2,1,0:T(8,128)(2,1)} custom-call(bf16[2,256,512]{2,1,0:T(8,128)(2,1)} %get-tuple-element.7.left_ref, bf16[512,1024]{1,0:T(8,128)(2,1)} %bitcast.1), custom_call_target="tpu_custom_call" | custom-call | tf_op jit(solution)/shard_map/pallas_call | solution.py:374
where the time goes:
time: 32 us; the launch traced here: 31.7 us
  Pallas kernels  30.4 us (95%)
  local copies, waits for them, and re-layouts  1.35 us (4%)
    pallas_call x1, Pallas kernels, focus(): pl.pallas_call(functools.partial(focus_kernel, n_pulse, n_tile, r_dev), o...  25.6 us
    pallas_call x1, Pallas kernels, image(): pl.pallas_call(image_kernel, grid=(band // width,), out_shape=jax.ShapeDt...  4.73 us
    unnamed x1, local copies, waits for them, and re-layouts  1.35 us

commit v1 on v0

--- a/solution.py
+++ b/solution.py
@@ -12,7 +12,7 @@
 MESH = pl.DeviceIdType.MESH
 LANES = 128
 DOP_SPLIT = 32
-VMEM_LIMIT = 60 * 1024 * 1024
+VMEM_LIMIT = 44 * 1024 * 1024
 
 
 def spread(meta, field, rows8, n_rows):
@@ -40,8 +40,8 @@
 def focus_kernel(
     n_pulse, n_tile, r_dev,
     off_ref, fine_ref, dop_ref, order_ref, idx_ref, raw_ref, filt_ref,
-    left_ref, bands_ref,
-    win_ref, meta_ref, scal_ref, filt_buf, x_ref, prof_ref, cut_ref, out_buf, g_ref, got_ref,
+    left_ref, samp_ref,
+    bands_ref, up_ref, win_ref, meta_ref, scal_ref, filt_buf, x_ref, prof_ref, cut_ref, out_buf, g_ref, got_ref,
     f_sem, s_sem, z_send, z_recv, t_send, t_recv, p_send, p_recv, g_send, g_recv,
 ):
     me_p = lax.axis_index("pulse")
@@ -105,8 +105,13 @@
         line = jnp.where(pulse_lane & (lane // rows8 == 3), dop_ref[p] // DOP_SPLIT, line)
         line = jnp.where((lane < rows8) & (lane % p_dev == order_ref[0, p]), p, line)
         for t in range(n_tile):
-            line = jnp.where(lane == 4 * rows8 + t * p_dev + p, idx_ref[t, p], line)
+            line = jnp.where(lane == 4 * rows8 + t * p_dev + p, idx_ref[p, t], line)
     meta_ref[core, mine] = line
+    j = lax.broadcasted_iota(jnp.int32, up_ref.shape, 0)
+    c = lax.broadcasted_iota(jnp.int32, up_ref.shape, 1)
+    w = (c % 4).astype(F32) * 0.25
+    up = jnp.where(j < LANES, 1.0 - w, w)
+    up_ref[...] = jnp.where(j % LANES == c // 4, up, 0.0).astype(BF16)
     pl.semaphore_wait(barrier, n_pulse - 1 + n_tile - 1)
 
     def copies(slot, send, recv, at, target):
@@ -168,7 +173,7 @@
             ]
         return carry
 
-    lax.fori_loop(0, chunks, compress, 0)
+    lax.fori_loop(0, chunks, compress, 0, unroll=2)
     to_scalar.wait()
     lane8 = lax.broadcasted_iota(jnp.int32, (pieces, LANES), 1)
 
@@ -279,6 +284,18 @@
     norm = 1.0 / jnp.sqrt(F32(n_rows // 2))
     er = (jnp.cos(angle) * norm).astype(BF16).astype(F32)
     ei = (jnp.sin(angle) * norm).astype(BF16).astype(F32)
+    square = (n_rows, n_rows)
+    diagonal = lax.broadcasted_iota(jnp.int32, square, 0) == lax.broadcasted_iota(jnp.int32, square, 1)
+    fine_col = jnp.sum(jnp.where(diagonal, fine, 0.0), axis=1, keepdims=True)
+    for s in range(pieces):
+        cols = slice(s * LANES, (s + 1) * LANES)
+        b0 = bands_ref[0, :, :, cols].reshape(n_rows, LANES).astype(F32)
+        b1 = bands_ref[1, :, :, cols].reshape(n_rows, LANES).astype(F32)
+        bend = fine_col * (b1 - b0)
+        pair = jnp.concatenate([b0 + bend, b1 + bend], 1).astype(BF16)
+        samp_ref[:, 4 * s * LANES : 4 * (s + 1) * LANES] = jnp.dot(
+            pair, up_ref[...], preferred_element_type=F32
+        ).astype(BF16)
     total = g_ref[...]
     for d in range(1, n_tile):
         g_moves[d - 1].wait_recv()
@@ -292,10 +309,7 @@
     w = (er * alpha - ei * beta, er * beta + ei * alpha)
     for z in range(2):
         here = pl.ds(z * r_dev, r_dev)
-        left_ref[0, here, :n_rows] = (w[z] * (1.0 - fine)).astype(BF16)
-        left_ref[0, here, n_rows:] = (w[z] * fine).astype(BF16)
-        left_ref[1, here, :n_rows] = (w[z] * -fine).astype(BF16)
-        left_ref[1, here, n_rows:] = (w[z] * (1.0 + fine)).astype(BF16)
+        left_ref[here, :] = w[z].astype(BF16)
     for c in started + [meta_move] + band_moves + g_moves:
         c.wait_send()
 
@@ -314,13 +328,15 @@
     return pl.pallas_call(
         functools.partial(focus_kernel, n_pulse, n_tile, r_dev),
         out_shape=(
-            jax.ShapeDtypeStruct((2, 2 * r_dev, 2 * n_rows), BF16),
-            jax.ShapeDtypeStruct((2, 2, rows, band), BF16),
+            jax.ShapeDtypeStruct((2 * r_dev, n_rows), BF16),
+            jax.ShapeDtypeStruct((n_rows, 4 * band), BF16),
         ),
         in_specs=[pl.BlockSpec(memory_space=pltpu.SMEM)] * 5
         + [pl.BlockSpec(memory_space=pltpu.VMEM), pl.BlockSpec(memory_space=pl.ANY)],
         out_specs=[pl.BlockSpec(memory_space=pltpu.VMEM)] * 2,
         scratch_shapes=[
+            pltpu.VMEM((2, 2, rows, band), BF16),
+            pltpu.VMEM((2 * LANES, 4 * LANES), BF16),
             pltpu.VMEM((n_dev, 2 * p_dev, win), BF16),
             pltpu.VMEM((2, n_dev, 1, width), jnp.int32),
             pltpu.SMEM((n_dev, 1, width), jnp.int32),
@@ -348,41 +364,27 @@
     )(range_off, fine, dop, order, idx, raw, filt)
 
 
-def image_kernel(left_ref, bands_ref, out_ref, up_ref):
+def image_kernel(left_ref, samp_ref, out_ref):
     r_dev = out_ref.shape[1]
-    width = bands_ref.shape[1]
-    out_chunk = 4 * LANES
-    j = lax.broadcasted_iota(jnp.int32, up_ref.shape, 0)
-    c = lax.broadcasted_iota(jnp.int32, up_ref.shape, 1)
-    w = (c % 4).astype(F32) * 0.25
-    up = jnp.where(j < LANES, 1.0 - w, w)
-    up_ref[...] = jnp.where(j % LANES == c // 4, up, 0.0).astype(BF16)
-    r0 = jnp.dot(left_ref[0], bands_ref[...], preferred_element_type=F32).astype(BF16)
-    r1 = jnp.dot(left_ref[1], bands_ref[...], preferred_element_type=F32).astype(BF16)
-    for s in range(width // LANES):
-        cols = slice(s * LANES, (s + 1) * LANES)
-        both = jnp.concatenate([r0[:, cols], r1[:, cols]], 1)
-        res = jnp.dot(both, up_ref[...], preferred_element_type=F32).astype(BF16)
-        for z in range(2):
-            out_ref[z, :, s * out_chunk : (s + 1) * out_chunk] = res[z * r_dev : (z + 1) * r_dev]
-
-
-def image(left, bands, r_dev):
-    band = bands.shape[1]
-    k = bands.shape[0]
-    width = 2 * LANES
+    res = jnp.dot(left_ref[...], samp_ref[...], preferred_element_type=F32).astype(BF16)
+    for z in range(2):
+        out_ref[z] = res[z * r_dev : (z + 1) * r_dev]
+
+
+def image(left, samples, r_dev):
+    k, cols = samples.shape
+    width = cols // 4
     return pl.pallas_call(
         image_kernel,
-        grid=(band // width,),
-        out_shape=jax.ShapeDtypeStruct((2, r_dev, 4 * band), BF16),
+        grid=(cols // width,),
+        out_shape=jax.ShapeDtypeStruct((2, r_dev, cols), BF16),
         in_specs=[
-            pl.BlockSpec(left.shape, lambda i: (0, 0, 0)),
+            pl.BlockSpec(left.shape, lambda i: (0, 0)),
             pl.BlockSpec((k, width), lambda i: (0, i)),
         ],
-        out_specs=pl.BlockSpec((2, r_dev, 4 * width), lambda i: (0, 0, i)),
-        scratch_shapes=[pltpu.VMEM((2 * LANES, 4 * LANES), BF16)],
+        out_specs=pl.BlockSpec((2, r_dev, width), lambda i: (0, 0, i)),
         compiler_params=pltpu.CompilerParams(vmem_limit_bytes=VMEM_LIMIT),
-    )(left, bands)
+    )(left, samples)
 
 
 BAND = 1024
@@ -392,11 +394,10 @@
 def shards(raw, filt, range_off, fine, dop, pulse_order, band_idx):
     n_pulse = lax.axis_size("pulse")
     n_tile = lax.axis_size("tile")
-    left, bands = focus(
-        n_pulse, n_tile, R_DEV, BAND, range_off, fine, dop, pulse_order, band_idx, raw, filt
+    left, samples = focus(
+        n_pulse, n_tile, R_DEV, BAND, range_off, fine, dop, pulse_order, band_idx.T, raw, filt
     )
-    bands = bands.reshape(-1, BAND)
-    return image(left, bands, R_DEV)
+    return image(left, samples, R_DEV)
 
 
 def solution(mesh):

time: 32 us -> 32 us (level)
  local copies, waits for them, and re-layouts: 1.35 us -> 4.06 us
  Pallas kernels: 30.4 us -> 27.7 us
    unnamed x1 -> x12, local copies, waits for them, and re-layouts: 1.35 us -> 4.06 us
    pallas_call x1, Pallas kernels: 4.73 us -> 2.65 us  [image(): pl.pallas_call(image_kernel, grid=(cols // width,), out_shape=jax.ShapeDt...]
    pallas_call x1, Pallas kernels: 25.6 us -> 25.1 us  [focus(): pl.pallas_call(functools.partial(focus_kernel, n_pulse, n_tile, r_dev), o...]
where the time goes in v1:
time: 32 us; the launch traced here: 31.8 us
  Pallas kernels  27.7 us (87%)
  local copies, waits for them, and re-layouts  4.06 us (13%)
    pallas_call x1, Pallas kernels, focus(): pl.pallas_call(functools.partial(focus_kernel, n_pulse, n_tile, r_dev), o...  25.1 us
    unnamed x12, local copies, waits for them, and re-layouts  4.06 us
    pallas_call x1, Pallas kernels, image(): pl.pallas_call(image_kernel, grid=(cols // width,), out_shape=jax.ShapeDt...  2.65 us

profile of v1, /device:TPU:0, one launch (start us, length us, event | category | flops | bytes accessed | tf_op | source)
XLA Modules:
  0.0 31.8 jit_solution(16691184026862576815)
XLA Ops:
  0.0 0.0 copy-start
  0.0 0.8 %copy-done = bf16[2,4,2048]{2,1,0:T(4,128)(2,1)S(1)} copy-done((bf16[2,4,2048]{2,1,0:T(4,128)(2,1)S(1)}, bf16[2,4,2048]{2,1,0:T(4,128)(2,1)}, u32[]{:S(2)}) %copy-start) | copy-done | bytes 32792
  0.8 0.0 copy-start.1
  0.8 0.7 %copy-done.1 = s32[8,4]{0,1:T(4,128)S(1)} copy-done((s32[8,4]{0,1:T(4,128)S(1)}, s32[8,4]{0,1:T(4,128)}, u32[]{:S(2)}) %copy-start.1) | copy-done | bytes 152
  1.4 0.0 copy-start.2
  1.4 0.7 %copy-done.2 = s32[4]{0:T(128)S(1)} copy-done((s32[4]{0:T(128)S(1)}, s32[4]{0:T(128)}, u32[]{:S(2)}) %copy-start.2) | copy-done | bytes 40
  2.1 0.0 copy-start.3
  2.1 0.7 %copy-done.3 = s32[4]{0:T(128)S(1)} copy-done((s32[4]{0:T(128)S(1)}, s32[4]{0:T(128)}, u32[]{:S(2)}) %copy-start.3) | copy-done | bytes 40
  2.8 0.0 copy-start.4
  2.8 0.7 %copy-done.4 = s32[4]{0:T(128)S(1)} copy-done((s32[4]{0:T(128)S(1)}, s32[4]{0:T(128)}, u32[]{:S(2)}) %copy-start.4) | copy-done | bytes 40
  3.4 0.0 copy-start.5
  3.4 0.7 %copy-done.5 = s32[1,4]{1,0:T(1,128)S(1)} copy-done((s32[1,4]{1,0:T(1,128)S(1)}, s32[1,4]{1,0:T(1,128)}, u32[]{:S(2)}) %copy-start.5) | copy-done | bytes 40
  4.1 25.1 %shard_map.73 = (bf16[256,256]{1,0:T(8,128)(2,1)S(1)}, bf16[256,4096]{1,0:T(8,128)(2,1)S(1)}) custom-call(s32[4]{0:T(128)S(1)} %copy-done.2, s32[4]{0:T(128)S(1)} %copy-done.3, s32[4]{0:T(128)S(1)} %copy-done.4, s32[1,4]{1,0:T(1,128)S(1)} %copy-done.5, s32[4,8]{1,0:T(4,128)S(1)} %bitcast.1, bf16[2,4,2048]{2,1,0:T(4,128)(2,1)S(1)} %copy-done, ...), custom_call_target="tpu_custom_call" | custom-call | tf_op jit(solution)/shard_map/pallas_call | solution.py:328
  29.2 2.6 %shard_map.74 = bf16[2,128,4096]{2,1,0:T(8,128)(2,1)} custom-call(bf16[256,256]{1,0:T(8,128)(2,1)S(1)} %get-tuple-element.7.left_ref, bf16[256,4096]{1,0:T(8,128)(2,1)S(1)} %get-tuple-element.8.samp_ref), custom_call_target="tpu_custom_call" | custom-call | tf_op jit(solution)/shard_map/pallas_call | solution.py:377
Async XLA Ops:
  0.0 0.8 %copy-start = (bf16[2,4,2048]{2,1,0:T(4,128)(2,1)S(1)}, bf16[2,4,2048]{2,1,0:T(4,128)(2,1)}, u32[]{:S(2)}) copy-start(bf16[2,4,2048]{2,1,0:T(4,128)(2,1)} %raw_ref.1) | copy-start | bytes 98308
  0.8 0.7 %copy-start.1 = (s32[8,4]{0,1:T(4,128)S(1)}, s32[8,4]{0,1:T(4,128)}, u32[]{:S(2)}) copy-start(s32[8,4]{0,1:T(4,128)} %param.13) | copy-start | bytes 388
  1.4 0.7 %copy-start.2 = (s32[4]{0:T(128)S(1)}, s32[4]{0:T(128)}, u32[]{:S(2)}) copy-start(s32[4]{0:T(128)} %off_ref.1) | copy-start | bytes 52
  2.1 0.7 %copy-start.3 = (s32[4]{0:T(128)S(1)}, s32[4]{0:T(128)}, u32[]{:S(2)}) copy-start(s32[4]{0:T(128)} %fine_ref.1) | copy-start | bytes 52
  2.8 0.7 %copy-start.4 = (s32[4]{0:T(128)S(1)}, s32[4]{0:T(128)}, u32[]{:S(2)}) copy-start(s32[4]{0:T(128)} %dop_ref.1) | copy-start | bytes 52
  3.4 0.7 %copy-start.5 = (s32[1,4]{1,0:T(1,128)S(1)}, s32[1,4]{1,0:T(1,128)}, u32[]{:S(2)}) copy-start(s32[1,4]{1,0:T(1,128)} %order_ref.1) | copy-start | bytes 52
